TPU v7x, 128 devices: a whole 4x4x4 slice. The times are simulated.
128 devices in a mesh: wide: 16 (over x_hi, z, core), narrow: 8 (over y, x_lo).
Axes of the slice: x: 4 (x_hi: 2, x_lo: 2; x = x_hi * 2 + x_lo), y: 4, z: 4, core: 2. Of those that a mesh axis runs over, the one named last changes fastest.
Arguments:
- block_states: bfloat16 [32, 64, 4096], P('wide', None, 'narrow'), may hold values from -6 to 6
- attn_gain: float32 [4096], replicated, may hold values from 0.1 to 1.9
- ffn_gain: float32 [4096], replicated, may hold values from 0.1 to 1.9
- final_gain: float32 [4096], replicated, may hold values from 0.1 to 1.9
- w_query: bfloat16 [4096, 4096], P(None, 'narrow'), may hold values from -0.09375 to 0.09375
- w_keyval: bfloat16 [4096, 1024], replicated, may hold values from -0.09375 to 0.09375
- w_out: bfloat16 [4096, 4096], P('narrow'), may hold values from -0.09375 to 0.09375
- w_gate: bfloat16 [4096, 1024], P(None, 'narrow'), may hold values from -0.09375 to 0.09375
- w_up: bfloat16 [4096, 1024], P(None, 'narrow'), may hold values from -0.09375 to 0.09375
- w_down: bfloat16 [1024, 4096], P('narrow'), may hold values from -0.1875 to 0.1875
- w_head: bfloat16 [4096, 131072], P(None, ('wide', 'narrow')), may hold values from -8 to 8
- cache: bfloat16 [32, 512, 4, 256], P('wide'), may hold values from -2000 to 2000
- prefix_lengths: int32 [32], P('wide'), may hold values from 128 to 512, as said below
- masked_positions: int32 [16, 64], replicated, may hold values from 0 to 63, as said below
Outputs:
- log_probs: float32 [1024, 131072], P(None, ('wide', 'narrow'))
- confidence: float32 [16, 64], replicated
Inputs may be any that keep to these rules, and one draw needn't show every extreme that they name: `prefix_lengths`: some request branch has exactly 512 valid positions. `masked_positions`: the 64 positions of one request are distinct.
All inputs are finite; a program needn't handle non-finite values.
Results may differ from a plain program's by a relative error of at most 0.024.
The roundings to bfloat16 on the way count: a program that leaves them out, or rounds other values in their place, can miss the bound.
Values may be sent and summed in bfloat16 or wider, within the bound.
No kernel may reach another device: no remote copies, remote signals or barrier semaphores. Data moves between devices by JAX's collectives and lax.ppermute only.
A program may use at most 128 MiB of HBM per device.

v0:
```python
import math
import jax
import jax.numpy as jnp
from jax import lax
from jax.sharding import PartitionSpec as P

KVH = 4
HD = 128
EPS = 1e-06
GUIDE = 1.5


def swapped(value, axis, bit):
    mask = 2**bit
    pairs = [(source, source ^ mask) for source in range(lax.axis_size(axis))]
    return lax.ppermute(value, axis, pairs)


def rms_scale(rows, gain):
    return rows * lax.rsqrt(jnp.mean(rows * rows, axis=-1, keepdims=True) + EPS) * gain


def split_halves(rows, is_upper, kept_count):
    lower_part = rows[:kept_count]
    upper_part = rows[kept_count:]
    outgoing = jnp.where(is_upper, lower_part, upper_part)
    own_rows = jnp.where(is_upper, upper_part, lower_part)
    return (outgoing, own_rows)


def guide_rows(own_rows, partner, is_upper):
    cond_rows = jnp.where(is_upper, partner, own_rows)
    uncond_rows = jnp.where(is_upper, own_rows, partner)
    return (uncond_rows + GUIDE * (cond_rows - uncond_rows)).astype(jnp.bfloat16)


def on_device(
    block_states,
    attn_gain,
    ffn_gain,
    final_gain,
    w_query,
    w_keyval,
    w_out,
    w_gate,
    w_up,
    w_down,
    w_head,
    cache,
    prefix_lengths,
    masked_positions,
):
    n_wide = lax.axis_size("wide")
    n_narrow = lax.axis_size("narrow")
    wide_index = lax.axis_index("wide")
    narrow_index = lax.axis_index("narrow")
    half_wide = n_wide // 2
    local_req = block_states.shape[0]
    kept_count = local_req // 2
    masked = masked_positions.shape[1]
    is_upper = wide_index >= half_wide
    full_rows = lax.all_gather(block_states, "narrow", axis=2, tiled=True)
    normed = rms_scale(full_rows.astype(jnp.float32), attn_gain).astype(jnp.bfloat16)
    kv_head = narrow_index // (n_narrow // KVH)
    head_weight = lax.dynamic_slice_in_dim(w_keyval, kv_head * (2 * HD), 2 * HD, 1)
    block_kv = jnp.einsum(
        "bld,dc->blc", normed, head_weight, preferred_element_type=jnp.float32
    ).astype(jnp.bfloat16)
    cache_kv = lax.dynamic_index_in_dim(cache, kv_head, axis=2, keepdims=False)
    first_req = wide_index % half_wide * local_req
    my_positions = lax.dynamic_slice_in_dim(masked_positions, first_req, local_req, 0)
    picked = jax.vmap(lambda rows, idx: rows[idx])(full_rows, my_positions)
    picked_normed = jax.vmap(lambda rows, idx: rows[idx])(normed, my_positions)
    local_heads = w_query.shape[1] // HD
    query = jnp.einsum(
        "bmd,dc->bmc", picked_normed, w_query, preferred_element_type=jnp.float32
    ).astype(jnp.bfloat16)
    query = query.reshape(local_req, masked, local_heads, HD)
    scale = 1.0 / math.sqrt(HD)
    pre_scores = (
        jnp.einsum("bmhd,bpd->bhmp", query, cache_kv[..., :HD], preferred_element_type=jnp.float32)
        * scale
    )
    live = jnp.arange(cache_kv.shape[1])[None, :] < prefix_lengths[:, None]
    pre_scores = jnp.where(live[:, None, None, :], pre_scores, -jnp.inf)
    blk_scores = (
        jnp.einsum("bmhd,bld->bhml", query, block_kv[..., :HD], preferred_element_type=jnp.float32)
        * scale
    )
    peak = jnp.maximum(
        jnp.max(pre_scores, axis=-1, keepdims=True), jnp.max(blk_scores, axis=-1, keepdims=True)
    )
    pre_weights = jnp.exp(pre_scores - peak)
    blk_weights = jnp.exp(blk_scores - peak)
    weight_total = jnp.sum(pre_weights, axis=-1, keepdims=True) + jnp.sum(
        blk_weights, axis=-1, keepdims=True
    )
    pre_probs = (pre_weights / weight_total).astype(jnp.bfloat16)
    blk_probs = (blk_weights / weight_total).astype(jnp.bfloat16)
    attended = jnp.einsum(
        "bhmp,bpd->bmhd", pre_probs, cache_kv[..., HD:], preferred_element_type=jnp.float32
    )
    attended = attended + jnp.einsum(
        "bhml,bld->bmhd", blk_probs, block_kv[..., HD:], preferred_element_type=jnp.float32
    )
    attended = attended.astype(jnp.bfloat16).reshape(local_req, masked, local_heads * HD)
    attn_part = jnp.einsum("bmc,cd->bmd", attended, w_out, preferred_element_type=jnp.float32)
    attn_total = lax.psum(attn_part, "narrow")
    first = picked.astype(jnp.float32) + attn_total
    ffn_in = rms_scale(first, ffn_gain).astype(jnp.bfloat16)
    gate_act = jnp.einsum("bmd,dc->bmc", ffn_in, w_gate, preferred_element_type=jnp.float32)
    up_act = jnp.einsum("bmd,dc->bmc", ffn_in, w_up, preferred_element_type=jnp.float32)
    hidden = (jax.nn.silu(gate_act) * up_act).astype(jnp.bfloat16)
    ffn_part = jnp.einsum("bmc,cd->bmd", hidden, w_down, preferred_element_type=jnp.float32)
    swap_bit = n_wide.bit_length() - 2
    vocab_cols = w_head.shape[1]
    ffn_total = lax.psum(ffn_part, "narrow")
    final = rms_scale(first + ffn_total, final_gain)
    outgoing, own_rows = split_halves(final, is_upper, kept_count)
    partner = swapped(outgoing, "wide", swap_bit)
    guided = guide_rows(own_rows, partner, is_upper).reshape(kept_count * masked, -1)
    logits = jnp.dot(
        lax.all_gather(guided, "wide", axis=0, tiled=True),
        w_head,
        preferred_element_type=jnp.float32,
    )
    logits = logits.reshape(2, half_wide, kept_count, masked, vocab_cols)
    logits = jnp.transpose(logits, (1, 0, 2, 3, 4)).reshape(-1, vocab_cols)
    local_peak = jnp.max(logits, axis=-1)
    row_peak = lax.pmax(local_peak, ("wide", "narrow"))
    row_total = lax.psum(jnp.sum(jnp.exp(logits - row_peak[:, None]), axis=-1), ("wide", "narrow"))
    lse = row_peak + jnp.log(row_total)
    log_probs = logits - lse[:, None]
    confidence = jnp.exp(row_peak - lse).reshape(-1, masked)
    return (log_probs, confidence)


def solution(mesh):
    in_specs = (
        P("wide", None, "narrow"),
        P(),
        P(),
        P(),
        P(None, "narrow"),
        P(),
        P("narrow", None),
        P(None, "narrow"),
        P(None, "narrow"),
        P("narrow", None),
        P(None, ("wide", "narrow")),
        P("wide", None, None, None),
        P("wide"),
        P(),
    )
    out_specs = (P(None, ("wide", "narrow")), P())
    return jax.shard_map(
        on_device, mesh=mesh, in_specs=in_specs, out_specs=out_specs, check_vma=False
    )
```

profile of v0, /device:TPU:1, one launch (start us, length us, event | category | flops | bytes accessed | tf_op | source)
XLA Modules:
  0.0 550.7 jit_solution(10640468757488981066)
XLA Ops:
  7.2 0.7 all-gather.4.cloned.1.call-update
  8.0 0.7 fusion.54
  8.7 0.1 reshape.99
  8.8 1.1 constant_dynamic-slice_fusion
  9.9 0.1 copy.68
  10.0 0.1 iota_compare_fusion
  10.1 38.0 %all-gather.4.cloned.1.call-done = bf16[2,64,4096]{2,1,0:T(8,128)(2,1)} async-done(((bf16[2,64,512]{2,1,0:T(8,128)(2,1)}), bf16[2,64,4096]{2,1,0:T(8,128)(2,1)}) %all-gather.4.cloned.1.call-update) | async-done | bytes 1048592 | tf_op jit(solution)/shard_map/all_gather | solution.py:62
  48.1 1.5 fusion.6
  49.6 1.6 fusion.8
  51.2 3.9 gather_fusion.1
  55.1 2.2 fusion.23
  57.2 0.6 copy-done.6
  57.9 0.8 fusion.19
  58.7 0.3 fusion.58
  58.9 0.4 fusion.57
  59.4 0.3 fusion.33
  59.7 0.4 fusion.35
  60.2 0.2 fusion.22
  60.4 1.5 copy-done.7
  61.9 2.1 fusion.2
  64.0 0.2 all-reduce.5.cloned.1.call-start
  64.3 1.0 copy-done.2
  65.2 3.9 gather_fusion
  69.1 103.4 %all-reduce.3.cloned.1.call-done = f32[2,64,4096]{2,1,0:T(8,128)} async-done(((f32[2,64,4096]{2,1,0:T(8,128)}), f32[2,64,4096]{2,1,0:T(8,128)}) %all-reduce.3.cloned.1.call-update) | async-done | bytes 2097168 | tf_op jit(solution)/shard_map/psum | solution.py:108
  172.5 2.1 multiply_reduce_fusion.1
  174.7 1.4 multiply_convert_fusion
  176.1 1.7 fusion.31
  177.8 4.0 fusion.27
  181.8 103.9 %all-reduce.5.cloned.1.call-done = f32[2,64,4096]{2,1,0:T(8,128)} async-done(((f32[2,64,4096]{2,1,0:T(8,128)}), f32[2,64,4096]{2,1,0:T(8,128)}) %all-reduce.5.cloned.1.call-update) | async-done | bytes 2097168 | tf_op jit(solution)/shard_map/psum | solution.py:117
  285.8 2.2 multiply_reduce_fusion
  288.0 0.6 multiply_multiply_fusion
  288.6 0.1 slice_select_fusion
  288.7 2.5 collective-permute-start
  291.2 22.3 %collective-permute-done = f32[1,64,4096]{2,1,0:T(8,128)S(1)} collective-permute-done((f32[1,64,4096]{2,1,0:T(8,128)S(1)}, f32[1,64,4096]{2,1,0:T(8,128)S(1)}, u32[]{:S(2)}, u32[]{:S(2)}) %collective-permute-start) | collective-permute-done | bytes 1048608 | tf_op jit(solution)/shard_map/ppermute | solution.py:16
  313.5 1.0 add_convert_fusion
  314.6 74.8 %all-gather.6.cloned.1.call-done = bf16[1,1024,4096]{2,1,0:T(8,128)(2,1)} async-done(((bf16[1,64,4096]{2,1,0:T(8,128)(2,1)}), bf16[1,1024,4096]{2,1,0:T(8,128)(2,1)}) %all-gather.6.cloned.1.call-update) | async-done | bytes 8388624 | tf_op jit(solution)/shard_map/all_gather | solution.py:123
  389.4 12.6 %fusion = f32[1024,1024]{1,0:T(8,128)S(1)} fusion(bf16[4096,1024]{1,0:T(8,128)(2,1)} %param.24, bf16[1,1024,4096]{2,1,0:T(8,128)(2,1)} %all-gather.6.cloned.1.call-done), kind=kOutput, calls=%fused_computation.2 | convolution fusion | flops 8589934592 | bytes 20971520 | tf_op jit(solution)/shard_map/dot_general | solution.py:122
  402.0 2.0 copy-done.3
  404.0 2.2 copy.39
  406.3 2.5 reduce_max.31
  408.8 0.1 reduce_max.32
  408.8 64.3 %pmax.7 = f32[1024]{0:T(1024)S(1)} all-reduce(f32[1024]{0:T(1024)S(1)} %reduce_max.32), channel_id=1, replica_groups=mesh['wide'=16,'narrow'=8] {'wide','narrow'}, use_global_device_ids=true, to_apply=%region_10.11 | all-reduce | flops 1024 | bytes 8192 | tf_op jit(solution)/shard_map/pmax | solution.py:130
  473.1 0.1 sub.51
  473.2 2.9 exponential_reduce_fusion
  476.2 0.1 reduce_sum.62
  476.2 62.5 %psum.23 = f32[1024]{0:T(1024)S(1)} all-reduce(f32[1024]{0:T(1024)S(1)} %reduce_sum.62), channel_id=1, replica_groups=mesh['wide'=16,'narrow'=8] {'wide','narrow'}, use_global_device_ids=true, to_apply=%region_12.13 | all-reduce | flops 1024 | bytes 8192 | tf_op jit(solution)/shard_map/psum | solution.py:131
  538.8 0.7 reshape.98
  539.4 4.7 bitcast_subtract_fusion
  (38 shorter events, 0.4 us)
Async XLA Ops:
  7.2 1.6 copy-start
  7.2 2.8 copy-start.12
  7.2 40.9 %all-gather.4.cloned.1.call-start = ((), (), s32[]{:S(2)}) async-start(), calls=%async_computation | async-start | bytes 1179648 | tf_op jit(solution)/shard_map/all_gather | solution.py:62
  7.9 164.6 %all-reduce.3.cloned.1.call-start = ((), (), s32[]{:S(2)}) async-start(), calls=%async_computation.1 | async-start | bytes 4194304 | tf_op jit(solution)/shard_map/psum | solution.py:108
  8.8 40.8 %copy-start.9 = (f32[4096]{0:T(1024)S(1)}, f32[4096]{0:T(1024)}, u32[]{:S(2)}) copy-start(f32[4096]{0:T(1024)} %param.15) | copy-start | bytes 49156
  55.0 2.8 copy-start.6
  59.7 2.2 copy-start.7
  64.0 1.2 copy-start.2
  64.0 221.7 %all-reduce.5.cloned.1.call-start = ((), (), s32[]{:S(2)}) async-start(), calls=%async_computation.2 | async-start | bytes 4194304 | tf_op jit(solution)/shard_map/psum | solution.py:117
  69.1 105.5 %copy-start.10 = (f32[4096]{0:T(1024)S(1)}, f32[4096]{0:T(1024)}, u32[]{:S(2)}) copy-start(f32[4096]{0:T(1024)} %param.16) | copy-start | bytes 49156
  172.5 2.2 copy-start.4
  174.7 1.4 copy-start.8
  181.8 207.7 %all-gather.6.cloned.1.call-start = ((), (), s32[]{:S(2)}) async-start(), calls=%async_computation.3 | async-start | bytes 8912896 | tf_op jit(solution)/shard_map/all_gather | solution.py:123
  181.8 106.2 %copy-start.11 = (f32[4096]{0:T(1024)S(1)}, f32[4096]{0:T(1024)}, u32[]{:S(2)}) copy-start(f32[4096]{0:T(1024)} %param.17) | copy-start | bytes 49156
  285.8 2.2 copy-start.5
  288.7 24.8 %collective-permute-start = (f32[1,64,4096]{2,1,0:T(8,128)S(1)}, f32[1,64,4096]{2,1,0:T(8,128)S(1)}, u32[]{:S(2)}, u32[]{:S(2)}) collective-permute-start(f32[1,64,4096]{2,1,0:T(8,128)S(1)} %slice_select_fusion), channel_id=1, source_target_pairs={{0,64},{8,72},{16,80},{24,88},{32,96},{40,104},{48,112},{56,120},{... | collective-permute-start | bytes 3145736 | tf_op jit(solution)/shard_map/ppermute | solution.py:16
  402.0 2.0 copy-start.3
  539.4 4.7 copy-start.1
Sparse Core Ops, SparseCore 0:
  9.6 38.3 all-gather.3
  64.1 108.3 all-reduce.2
  181.9 103.8 all-reduce.4
  314.7 74.6 all-gather.5
where the time goes:
time: 551 us
  waiting for transfers between devices  343 us (62%)
  blocking collectives  127 us (23%)
  matrix products  24.6 us (4%)
  other arithmetic  21.8 us (4%)
  local copies, waits for them, and re-layouts  17.4 us (3%)
  between operations  14 us (3%)
    psum x1, waiting for transfers between devices, on_device(): ffn_total = lax.psum(ffn_part, 'narrow')  104 us
    psum x1, waiting for transfers between devices, on_device(): attn_total = lax.psum(attn_part, 'narrow')  103 us
    all_gather x1, waiting for transfers between devices, on_device(): lax.all_gather(guided, 'wide', axis=0, tiled=True)  74.8 us
    pmax x1, blocking collectives, on_device(): row_peak = lax.pmax(local_peak, ('wide', 'narrow'))  64.3 us
    psum x1, blocking collectives, on_device(): lax.psum(jnp.sum(jnp.exp(logits - row_peak[:, None]), axis=-1), ('wide',...  62.5 us
    all_gather x1, waiting for transfers between devices, on_device(): full_rows = lax.all_gather(block_states, 'narrow', axis=2, tiled=True)  38 us
    ppermute x1, waiting for transfers between devices, swapped(): return lax.ppermute(value, axis, pairs)  22.3 us
    dot_general x1, matrix products, on_device(): jnp.dot(lax.all_gather(guided, 'wide', axis=0, tiled=True), w_head, prefe...  12.6 us
  transfers between devices with their start and end apart: 5, of which 5 were waited for; matrix products, arithmetic and copies ran while one was open for 1% of the time, Pallas kernels for 0%

commit v1 on v0

--- a/solution.py
+++ b/solution.py
@@ -59,7 +59,7 @@
     kept_count = local_req // 2
     masked = masked_positions.shape[1]
     is_upper = wide_index >= half_wide
-    full_rows = lax.all_gather(block_states, "narrow", axis=2, tiled=True)
+    full_rows = jnp.concatenate(lax.all_gather(block_states, "narrow"), axis=2)
     normed = rms_scale(full_rows.astype(jnp.float32), attn_gain).astype(jnp.bfloat16)
     kv_head = narrow_index // (n_narrow // KVH)
     head_weight = lax.dynamic_slice_in_dim(w_keyval, kv_head * (2 * HD), 2 * HD, 1)

time: 551 us -> 553 us (level)
  no operation moved by 1% of the time
where the time goes in v1:
time: 553 us; the launch traced here: 552 us
  waiting for transfers between devices  343 us (62%)
  blocking collectives  127 us (23%)
  matrix products  24.5 us (4%)
  other arithmetic  21.1 us (4%)
  local copies, waits for them, and re-layouts  19.6 us (4%)
  between operations  14 us (3%)
    psum x1, waiting for transfers between devices, on_device(): attn_total = lax.psum(attn_part, 'narrow')  104 us
    psum x1, waiting for transfers between devices, on_device(): ffn_total = lax.psum(ffn_part, 'narrow')  104 us
    all_gather x1, waiting for transfers between devices, on_device(): lax.all_gather(guided, 'wide', axis=0, tiled=True)  74.8 us
    pmax x1, blocking collectives, on_device(): row_peak = lax.pmax(local_peak, ('wide', 'narrow'))  64.3 us
    psum x1, blocking collectives, on_device(): lax.psum(jnp.sum(jnp.exp(logits - row_peak[:, None]), axis=-1), ('wide',...  62.5 us
    all_gather x1, waiting for transfers between devices, on_device(): full_rows = jnp.concatenate(lax.all_gather(block_states, 'narrow'), axis=2)  37.2 us
    ppermute x1, waiting for transfers between devices, swapped(): return lax.ppermute(value, axis, pairs)  22.3 us
    dot_general x1, matrix products, on_device(): jnp.dot(lax.all_gather(guided, 'wide', axis=0, tiled=True), w_head, prefe...  12.6 us
  transfers between devices with their start and end apart: 5, of which 5 were waited for; matrix products, arithmetic and copies ran while one was open for 1% of the time, Pallas kernels for 0%

profile of v1, /device:TPU:1, one launch (start us, length us, event | category | flops | bytes accessed | tf_op | source)
XLA Modules:
  0.0 552.3 jit_solution(10762993623698289507)
XLA Ops:
  7.2 0.7 all-gather.5.cloned.1.call-update
  8.0 0.7 fusion.51
  8.7 0.1 reshape.107
  8.8 1.1 constant_dynamic-slice_fusion
  9.9 0.9 copy.76
  10.8 37.2 %all-gather.5.cloned.1.call-done = bf16[16,64,512]{2,1,0:T(8,128)(2,1)} async-done(((bf16[2,64,512]{2,1,0:T(8,128)(2,1)}), bf16[16,64,512]{2,1,0:T(8,128)(2,1)}) %all-gather.5.cloned.1.call-update) | async-done | bytes 1048592 | tf_op jit(solution)/shard_map/all_gather | solution.py:62
  48.0 2.0 multiply_reduce_fusion.2
  50.1 1.8 copy.75
  51.9 0.5 reshape.100
  52.5 0.3 multiply_convert_fusion.1
  52.8 3.9 gather_fusion.1
  56.7 2.2 fusion.20
  58.9 0.6 copy-done.5
  59.5 0.7 fusion.16
  60.2 0.3 fusion.55
  60.6 0.4 fusion.54
  61.0 0.3 fusion.30
  61.4 0.4 fusion.32
  61.8 0.2 fusion.19
  62.1 1.5 copy-done.6
  63.6 2.1 fusion.2
  65.7 0.2 all-reduce.5.cloned.1.call-start
  65.9 3.9 gather_fusion
  69.8 104.3 %all-reduce.3.cloned.1.call-done = f32[2,64,4096]{2,1,0:T(8,128)} async-done(((f32[2,64,4096]{2,1,0:T(8,128)}), f32[2,64,4096]{2,1,0:T(8,128)}) %all-reduce.3.cloned.1.call-update) | async-done | bytes 2097168 | tf_op jit(solution)/shard_map/psum | solution.py:108
  174.1 2.1 multiply_reduce_fusion.1
  176.3 1.4 multiply_convert_fusion
  177.7 1.7 fusion.28
  179.4 4.0 fusion.24
  183.5 103.9 %all-reduce.5.cloned.1.call-done = f32[2,64,4096]{2,1,0:T(8,128)} async-done(((f32[2,64,4096]{2,1,0:T(8,128)}), f32[2,64,4096]{2,1,0:T(8,128)}) %all-reduce.5.cloned.1.call-update) | async-done | bytes 2097168 | tf_op jit(solution)/shard_map/psum | solution.py:117
  287.4 2.2 multiply_reduce_fusion
  289.6 0.6 multiply_multiply_fusion
  290.2 0.1 slice_select_fusion
  290.3 2.5 collective-permute-start
  292.8 22.3 %collective-permute-done = f32[1,64,4096]{2,1,0:T(8,128)S(1)} collective-permute-done((f32[1,64,4096]{2,1,0:T(8,128)S(1)}, f32[1,64,4096]{2,1,0:T(8,128)S(1)}, u32[]{:S(2)}, u32[]{:S(2)}) %collective-permute-start) | collective-permute-done | bytes 1048608 | tf_op jit(solution)/shard_map/ppermute | solution.py:16
  315.2 1.0 add_convert_fusion
  316.2 74.8 %all-gather.7.cloned.1.call-done = bf16[1,1024,4096]{2,1,0:T(8,128)(2,1)} async-done(((bf16[1,64,4096]{2,1,0:T(8,128)(2,1)}), bf16[1,1024,4096]{2,1,0:T(8,128)(2,1)}) %all-gather.7.cloned.1.call-update) | async-done | bytes 8388624 | tf_op jit(solution)/shard_map/all_gather | solution.py:123
  391.1 12.6 %fusion = f32[1024,1024]{1,0:T(8,128)S(1)} fusion(bf16[4096,1024]{1,0:T(8,128)(2,1)} %param.24, bf16[1,1024,4096]{2,1,0:T(8,128)(2,1)} %all-gather.7.cloned.1.call-done), kind=kOutput, calls=%fused_computation.2 | convolution fusion | flops 8589934592 | bytes 20971520 | tf_op jit(solution)/shard_map/dot_general | solution.py:122
  403.7 2.0 copy-done.2
  405.7 2.2 copy.43
  407.9 2.5 reduce_max.31
  410.4 0.1 reduce_max.32
  410.5 64.3 %pmax.7 = f32[1024]{0:T(1024)S(1)} all-reduce(f32[1024]{0:T(1024)S(1)} %reduce_max.32), channel_id=1, replica_groups=mesh['wide'=16,'narrow'=8] {'wide','narrow'}, use_global_device_ids=true, to_apply=%region_10.11 | all-reduce | flops 1024 | bytes 8192 | tf_op jit(solution)/shard_map/pmax | solution.py:130
  474.8 0.1 sub.51
  474.9 2.9 exponential_reduce_fusion
  477.8 0.1 reduce_sum.62
  477.9 62.5 %psum.23 = f32[1024]{0:T(1024)S(1)} all-reduce(f32[1024]{0:T(1024)S(1)} %reduce_sum.62), channel_id=1, replica_groups=mesh['wide'=16,'narrow'=8] {'wide','narrow'}, use_global_device_ids=true, to_apply=%region_12.13 | all-reduce | flops 1024 | bytes 8192 | tf_op jit(solution)/shard_map/psum | solution.py:131
  540.4 0.7 reshape.106
  541.1 4.7 bitcast_subtract_fusion
  (40 shorter events, 0.5 us)
Async XLA Ops:
  7.2 1.6 copy-start
  7.2 3.6 copy-start.12
  7.2 40.9 %all-gather.5.cloned.1.call-start = ((), (), s32[]{:S(2)}) async-start(), calls=%async_computation.2 | async-start | bytes 1179648 | tf_op jit(solution)/shard_map/all_gather | solution.py:62
  7.9 166.2 %all-reduce.3.cloned.1.call-start = ((), (), s32[]{:S(2)}) async-start(), calls=%async_computation | async-start | bytes 4194304 | tf_op jit(solution)/shard_map/psum | solution.py:108
  50.1 2.4 copy-start.9
  56.7 2.8 copy-start.5
  59.5 1.0 copy-start.8
  61.4 2.2 copy-start.6
  65.7 221.7 %all-reduce.5.cloned.1.call-start = ((), (), s32[]{:S(2)}) async-start(), calls=%async_computation.1 | async-start | bytes 4194304 | tf_op jit(solution)/shard_map/psum | solution.py:117
  69.8 106.5 %copy-start.10 = (f32[4096]{0:T(1024)S(1)}, f32[4096]{0:T(1024)}, u32[]{:S(2)}) copy-start(f32[4096]{0:T(1024)} %param.16) | copy-start | bytes 49156
  174.1 2.2 copy-start.3
  176.3 1.4 copy-start.7
  183.4 207.6 %all-gather.7.cloned.1.call-start = ((), (), s32[]{:S(2)}) async-start(), calls=%async_computation.3 | async-start | bytes 8912896 | tf_op jit(solution)/shard_map/all_gather | solution.py:123
  183.5 106.2 %copy-start.11 = (f32[4096]{0:T(1024)S(1)}, f32[4096]{0:T(1024)}, u32[]{:S(2)}) copy-start(f32[4096]{0:T(1024)} %param.17) | copy-start | bytes 49156
  287.4 2.2 copy-start.4
  290.3 24.8 %collective-permute-start = (f32[1,64,4096]{2,1,0:T(8,128)S(1)}, f32[1,64,4096]{2,1,0:T(8,128)S(1)}, u32[]{:S(2)}, u32[]{:S(2)}) collective-permute-start(f32[1,64,4096]{2,1,0:T(8,128)S(1)} %slice_select_fusion), channel_id=1, source_target_pairs={{0,64},{8,72},{16,80},{24,88},{32,96},{40,104},{48,112},{56,120},{... | collective-permute-start | bytes 3145736 | tf_op jit(solution)/shard_map/ppermute | solution.py:16
  403.7 2.0 copy-start.2
  541.1 4.7 copy-start.1
Sparse Core Ops, SparseCore 0:
  9.6 38.3 all-gather.4
  65.8 108.2 all-reduce.2
  183.5 103.8 all-reduce.4
  316.4 74.6 all-gather.6
